TPU v7x, 32 devices: a whole 2x2x4 slice. The times are simulated.
32 devices in a mesh: groups: 2 (over x), pb: 8 (over z, y), ka: 2 (over core).
Axes of the slice: x: 2, y: 2, z: 4, core: 2. Of those that a mesh axis runs over, the one named last changes fastest.
Arguments:
- queries: bfloat16 [12288, 256], P(('groups', 'pb', 'ka')), parts along dimension 0, may hold values from -6 to 6
- keys: bfloat16 [12288, 256], P(('groups', 'pb', 'ka')), parts along dimension 0, may hold values from -6 to 6
- values: bfloat16 [12288, 256], P(('groups', 'pb', 'ka')), parts along dimension 0, may hold values from -96 to 96
- block_pairs: int32 [4, 8, 16, 9], P('groups', 'pb'), parts along dimension 0, may hold values from -1 to 17
Outputs:
- attended: bfloat16 [12288, 256], P(('groups', 'pb', 'ka')), parts along dimension 0
There are 2 independent parts, one for each index of `groups`. A program takes and returns all parts, laid end to end along the dimension named above; each array names one. Nothing has to cross between parts.
Inputs may be any that keep to these rules, and one draw needn't show every extreme that they name: Every query block's pair with the key block of the same tokens is kept for every head.
All inputs are finite; a program needn't handle non-finite values.
Results may differ from a plain program's by a relative error of at most 0.0085.
Values may be sent and summed in bfloat16 or wider, within the bound.
A program may use at most 128 MiB of HBM per device.

v0:
```python
import jax
import jax.numpy as jnp
from jax import lax
from jax.sharding import PartitionSpec as P

HEAD = 128
HEADS = 2
BLOCK = 128
TOK_DEV = 384


NEGATIVE_FILL = -1e30


def head_major(rows, head_count):
    block_count = rows.shape[0] // BLOCK
    return rows.reshape(block_count, BLOCK, head_count, HEAD).transpose(2, 0, 1, 3)


def pick_blocks(blocks, index):
    return jnp.take_along_axis(blocks, index[:, :, None, None], axis=1)


def attend_shard(state_in, key_blocks, value_blocks, query_blocks, pair_codes):
    peak_run, total_run, accum_run = state_in
    head_count = pair_codes.shape[0]
    tile_blocks = query_blocks.shape[1]
    shard_blocks = key_blocks.shape[1]
    active = pair_codes >= 0
    clean = jnp.where(active, pair_codes, 0)
    query_index = clean // shard_blocks
    key_index = clean % shard_blocks
    head_numbers = jnp.arange(head_count)[None, :]
    query_sel = pick_blocks(query_blocks, query_index)
    key_sel = pick_blocks(key_blocks, key_index)
    value_sel = pick_blocks(value_blocks, key_index)
    scores = jnp.einsum(
        "hsqd,hskd->hsqk", query_sel, key_sel, preferred_element_type=jnp.float32
    ) * HEAD ** (-0.5)
    scores = jnp.where(active[:, :, None, None], scores, NEGATIVE_FILL)
    slot_max = scores.max(-1)
    is_kept_pair = (query_index[:, :, None] == jnp.arange(tile_blocks)[None, None, :]) & active[
        :, :, None
    ]
    block_max = jnp.where(is_kept_pair[..., None], slot_max[:, :, None, :], NEGATIVE_FILL).max(1)
    peak_new = jnp.maximum(peak_run, block_max.transpose(1, 0, 2))
    slot_peak = peak_new[query_index.T, head_numbers].transpose(1, 0, 2)
    chances = jnp.where(active[:, :, None, None], jnp.exp(scores - slot_peak[..., None]), 0.0)
    softmax_weight = chances.astype(jnp.bfloat16)
    pair_flag = is_kept_pair.astype(jnp.float32)
    added_total = jnp.einsum(
        "hsb,hsq->bhq", pair_flag, chances.sum(-1), precision=lax.Precision.HIGHEST
    )
    partial_output = jnp.einsum(
        "hsqk,hskd->hsqd", softmax_weight, value_sel, preferred_element_type=jnp.float32
    )
    added_accum = jnp.einsum(
        "hsb,hsqd->bhqd", pair_flag, partial_output, precision=lax.Precision.HIGHEST
    )
    rescale = jnp.exp(peak_run - peak_new)
    total_new = rescale * total_run + added_total
    accum_new = rescale[..., None] * accum_run + added_accum
    return (peak_new, total_new, accum_new)


def shard_folder(query_blocks, pair_table, partition_blocks):

    def fold_piece(state_in, piece, start):
        key_piece, value_piece = piece
        piece_count = key_piece.shape[1] // partition_blocks
        first_shard = start // partition_blocks

        def one_shard(offset, state_now):
            key_blocks = lax.dynamic_slice_in_dim(
                key_piece, offset * partition_blocks, partition_blocks, 1
            )
            value_blocks = lax.dynamic_slice_in_dim(
                value_piece, offset * partition_blocks, partition_blocks, 1
            )
            pair_codes = lax.dynamic_index_in_dim(pair_table, offset, 1, keepdims=False)
            return attend_shard(state_now, key_blocks, value_blocks, query_blocks, pair_codes)

        return lax.fori_loop(0, piece_count, one_shard, state_in)

    return fold_piece


def empty_state(tile_blocks, head_count):
    peak_start = jnp.full((tile_blocks, head_count, BLOCK), NEGATIVE_FILL, jnp.float32)
    total_start = jnp.zeros((tile_blocks, head_count, BLOCK), jnp.float32)
    accum_start = jnp.zeros((tile_blocks, head_count, BLOCK, HEAD), jnp.float32)
    return (peak_start, total_start, accum_start)


def finish_rows(accum_end, total_end):
    row_blocks = accum_end.shape[0]
    head_count = accum_end.shape[1]
    finished = (accum_end / total_end[..., None]).astype(jnp.bfloat16)
    return finished.transpose(0, 2, 1, 3).reshape(row_blocks * BLOCK, head_count * HEAD)


def local(queries, keys, values, block_pairs):
    column = lax.axis_index("ka")
    tile_count = lax.axis_size("pb")
    column_count = lax.axis_size("ka")
    shard_blocks = TOK_DEV // BLOCK
    tile_blocks = column_count * shard_blocks
    pair_table = lax.dynamic_index_in_dim(
        block_pairs[:, 0].reshape(HEADS, tile_count, column_count, -1), column, 2, keepdims=False
    )
    query_tile = lax.all_gather(queries, "ka", axis=0, tiled=True)
    query_blocks = head_major(query_tile, HEADS)
    key_blocks = head_major(keys, HEADS)
    value_blocks = head_major(values, HEADS)
    shard_fold = shard_folder(query_blocks, pair_table, shard_blocks)
    peak_end, total_end, accum_end = shard_fold(
        empty_state(tile_blocks, HEADS),
        (
            lax.all_gather(key_blocks, "pb", axis=1, tiled=True),
            lax.all_gather(value_blocks, "pb", axis=1, tiled=True),
        ),
        jnp.int32(0),
    )
    peaks, totals, accums = (
        lax.all_to_all(peak_end[None], "ka", split_axis=1, concat_axis=0, tiled=True),
        lax.all_to_all(total_end[None], "ka", split_axis=1, concat_axis=0, tiled=True),
        lax.all_to_all(accum_end[None], "ka", split_axis=1, concat_axis=0, tiled=True),
    )
    peak_top = peaks.max(0)
    factor = jnp.exp(peaks - peak_top)
    merged_total = (factor * totals).sum(0)
    merged = (factor[..., None] * accums).sum(0)
    return finish_rows(merged, merged_total)


def solution(mesh):
    in_specs = (
        P(("groups", "pb", "ka"), None),
        P(("groups", "pb", "ka"), None),
        P(("groups", "pb", "ka"), None),
        P("groups", "pb", None, None),
    )
    out_specs = P(("groups", "pb", "ka"), None)
    return jax.shard_map(local, mesh=mesh, in_specs=in_specs, out_specs=out_specs, check_vma=False)
```

profile of v0, /device:TPU:0, one launch (start us, length us, event | category | flops | bytes accessed | tf_op | source)
XLA Modules:
  0.0 210.9 jit_solution(7228367942312670010)
XLA Ops:
  6.5 1.0 reshape.223
  8.3 1.0 reshape.224
  10.2 2.2 %all_gather.9 = bf16[768,256]{1,0:T(8,128)(2,1)S(1)} all-gather(bf16[384,256]{1,0:T(8,128)(2,1)S(1)} %copy-done), channel_id=1, replica_groups=mesh['groups'=2,'pb'=8,'ka'=2] {'ka'}, dimensions={0}, use_global_device_ids=true | all-gather | bytes 589824 | tf_op jit(solution)/shard_map/all_gather | solution.py:111
  12.6 43.9 %all-gather.3.cloned.1.call-done = bf16[2,24,128,128]{3,2,0,1:T(8,128)(2,1)} async-done(((bf16[2,3,128,128]{3,2,0,1:T(8,128)(2,1)}), bf16[2,24,128,128]{3,2,0,1:T(8,128)(2,1)}) %all-gather.3.cloned.1.call-update) | async-done | bytes 1572880 | tf_op jit(solution)/shard_map/all_gather | solution.py:119
  56.5 44.8 %all-gather.5.cloned.1.call-done = bf16[2,24,128,128]{3,2,0,1:T(8,128)(2,1)} async-done(((bf16[2,3,128,128]{3,2,0,1:T(8,128)(2,1)}), bf16[2,24,128,128]{3,2,0,1:T(8,128)(2,1)}) %all-gather.5.cloned.1.call-update) | async-done | bytes 1572880 | tf_op jit(solution)/shard_map/all_gather | solution.py:120
  101.2 84.8 %while.20 = (s32[]{:T(128)}, f32[6,2,128]{2,0,1:T(8,128)S(1)}, f32[6,2,128]{2,0,1:T(8,128)S(1)}, f32[6,2,128,128]{3,0,2,1:T(8,128)}, s32[2,8,9]{2,1,0:T(8,128)S(...) while((s32[]{:T(128)}, f32[6,2,128]{2,0,1:T(8,128)S(1)}, ...), condition=%wide.region_4.6_spmd.clone, body=%wide.region_0.5_spmd.clone.sunk | while | flops 176555712 | bytes 14564423 | solution.py:83
  101.4 1.1 constant_dynamic-slice_fusion.7
  106.3 0.7 gather_fusion.3
  107.8 3.0 %fusion.70 = f32[6,2,128,128]{3,0,2,1:T(8,128)} fusion(f32[2,9,128,128]{3,2,1,0:T(8,128)S(1)} %fusion.69, f32[6,2,128,128]{3,0,2,1:T(8,128)} %get-tuple-element.411, f32[6,2,128]{0,2,1:T(8,128)S(1)} %copy.154, pred[]{:T(512)S(6)} %compare.3, s32[2,9]{1,0:T(2,128)S(1)} %get-tuple-element.382, pred[2,9]{1,0:T(4,128)(4,1)S(1)} %get-tuple-element.383), kind=kOutput, calls=%fused_computation.9.clone.1 | convolution fusion | flops 21823704 | bytes 2758747 | tf_op jit(solution)/shard_map/while/body/eval_jaxpr/hsb,hsqd->bhqd/dot_general | solution.py:57
  111.0 1.1 constant_dynamic-slice_fusion.7
  117.3 4.2 %fusion.70 = f32[6,2,128,128]{3,0,2,1:T(8,128)} fusion(f32[2,9,128,128]{3,2,1,0:T(8,128)S(1)} %fusion.69, f32[6,2,128,128]{3,0,2,1:T(8,128)} %get-tuple-element.411, f32[6,2,128]{0,2,1:T(8,128)S(1)} %copy.154, pred[]{:T(512)S(6)} %compare.3, s32[2,9]{1,0:T(2,128)S(1)} %get-tuple-element.382, pred[2,9]{1,0:T(4,128)(4,1)S(1)} %get-tuple-element.383), kind=kOutput, calls=%fused_computation.9.clone.1 | convolution fusion | flops 21823704 | bytes 2758747 | tf_op jit(solution)/shard_map/while/body/eval_jaxpr/hsb,hsqd->bhqd/dot_general | solution.py:57
  121.7 1.1 constant_dynamic-slice_fusion.7
  126.6 0.7 gather_fusion.3
  128.1 4.2 %fusion.70 = f32[6,2,128,128]{3,0,2,1:T(8,128)} fusion(f32[2,9,128,128]{3,2,1,0:T(8,128)S(1)} %fusion.69, f32[6,2,128,128]{3,0,2,1:T(8,128)} %get-tuple-element.411, f32[6,2,128]{0,2,1:T(8,128)S(1)} %copy.154, pred[]{:T(512)S(6)} %compare.3, s32[2,9]{1,0:T(2,128)S(1)} %get-tuple-element.382, pred[2,9]{1,0:T(4,128)(4,1)S(1)} %get-tuple-element.383), kind=kOutput, calls=%fused_computation.9.clone.1 | convolution fusion | flops 21823704 | bytes 2758747 | tf_op jit(solution)/shard_map/while/body/eval_jaxpr/hsb,hsqd->bhqd/dot_general | solution.py:57
  132.5 1.1 constant_dynamic-slice_fusion.7
  138.8 4.2 %fusion.70 = f32[6,2,128,128]{3,0,2,1:T(8,128)} fusion(f32[2,9,128,128]{3,2,1,0:T(8,128)S(1)} %fusion.69, f32[6,2,128,128]{3,0,2,1:T(8,128)} %get-tuple-element.411, f32[6,2,128]{0,2,1:T(8,128)S(1)} %copy.154, pred[]{:T(512)S(6)} %compare.3, s32[2,9]{1,0:T(2,128)S(1)} %get-tuple-element.382, pred[2,9]{1,0:T(4,128)(4,1)S(1)} %get-tuple-element.383), kind=kOutput, calls=%fused_computation.9.clone.1 | convolution fusion | flops 21823704 | bytes 2758747 | tf_op jit(solution)/shard_map/while/body/eval_jaxpr/hsb,hsqd->bhqd/dot_general | solution.py:57
  143.2 1.1 constant_dynamic-slice_fusion.7
  149.6 4.2 %fusion.70 = f32[6,2,128,128]{3,0,2,1:T(8,128)} fusion(f32[2,9,128,128]{3,2,1,0:T(8,128)S(1)} %fusion.69, f32[6,2,128,128]{3,0,2,1:T(8,128)} %get-tuple-element.411, f32[6,2,128]{0,2,1:T(8,128)S(1)} %copy.154, pred[]{:T(512)S(6)} %compare.3, s32[2,9]{1,0:T(2,128)S(1)} %get-tuple-element.382, pred[2,9]{1,0:T(4,128)(4,1)S(1)} %get-tuple-element.383), kind=kOutput, calls=%fused_computation.9.clone.1 | convolution fusion | flops 21823704 | bytes 2758747 | tf_op jit(solution)/shard_map/while/body/eval_jaxpr/hsb,hsqd->bhqd/dot_general | solution.py:57
  154.0 1.1 constant_dynamic-slice_fusion.7
  160.3 4.2 %fusion.70 = f32[6,2,128,128]{3,0,2,1:T(8,128)} fusion(f32[2,9,128,128]{3,2,1,0:T(8,128)S(1)} %fusion.69, f32[6,2,128,128]{3,0,2,1:T(8,128)} %get-tuple-element.411, f32[6,2,128]{0,2,1:T(8,128)S(1)} %copy.154, pred[]{:T(512)S(6)} %compare.3, s32[2,9]{1,0:T(2,128)S(1)} %get-tuple-element.382, pred[2,9]{1,0:T(4,128)(4,1)S(1)} %get-tuple-element.383), kind=kOutput, calls=%fused_computation.9.clone.1 | convolution fusion | flops 21823704 | bytes 2758747 | tf_op jit(solution)/shard_map/while/body/eval_jaxpr/hsb,hsqd->bhqd/dot_general | solution.py:57
  164.8 1.1 constant_dynamic-slice_fusion.7
  169.7 0.7 gather_fusion.3
  171.1 4.2 %fusion.70 = f32[6,2,128,128]{3,0,2,1:T(8,128)} fusion(f32[2,9,128,128]{3,2,1,0:T(8,128)S(1)} %fusion.69, f32[6,2,128,128]{3,0,2,1:T(8,128)} %get-tuple-element.411, f32[6,2,128]{0,2,1:T(8,128)S(1)} %copy.154, pred[]{:T(512)S(6)} %compare.3, s32[2,9]{1,0:T(2,128)S(1)} %get-tuple-element.382, pred[2,9]{1,0:T(4,128)(4,1)S(1)} %get-tuple-element.383), kind=kOutput, calls=%fused_computation.9.clone.1 | convolution fusion | flops 21823704 | bytes 2758747 | tf_op jit(solution)/shard_map/while/body/eval_jaxpr/hsb,hsqd->bhqd/dot_general | solution.py:57
  175.5 1.1 constant_dynamic-slice_fusion.7
  180.4 0.7 gather_fusion.3
  181.8 4.2 %fusion.70 = f32[6,2,128,128]{3,0,2,1:T(8,128)} fusion(f32[2,9,128,128]{3,2,1,0:T(8,128)S(1)} %fusion.69, f32[6,2,128,128]{3,0,2,1:T(8,128)} %get-tuple-element.411, f32[6,2,128]{0,2,1:T(8,128)S(1)} %copy.154, pred[]{:T(512)S(6)} %compare.3, s32[2,9]{1,0:T(2,128)S(1)} %get-tuple-element.382, pred[2,9]{1,0:T(4,128)(4,1)S(1)} %get-tuple-element.383), kind=kOutput, calls=%fused_computation.9.clone.1 | convolution fusion | flops 21823704 | bytes 2758747 | tf_op jit(solution)/shard_map/while/body/eval_jaxpr/hsb,hsqd->bhqd/dot_general | solution.py:57
  186.1 2.3 %copy.133 = f32[6,2,128,128]{3,2,1,0:T(8,128)} copy(f32[6,2,128,128]{3,0,2,1:T(8,128)} %get-tuple-element.210) | data formatting | bytes 1572864 | tf_op jit(solution)/shard_map/while | solution.py:83
  188.9 3.7 %all_to_all.36 = f32[1,6,2,128]{3,2,0,1:T(2,128)S(1)} all-to-all(f32[1,6,2,128]{3,2,0,1:T(2,128)S(1)} %bitcast.120), channel_id=1, replica_groups=mesh['groups'=2,'pb'=8,'ka'=2] {'ka'}, dimensions={1} | all-to-all | bytes 12288 | tf_op jit(solution)/shard_map/all_to_all | solution.py:125
  192.6 3.2 %all-to-all-start.2 = ((f32[1,6,2,128]{3,2,0,1:T(2,128)}), f32[1,6,2,128]{3,2,0,1:T(2,128)S(1)}, u32[]{:S(2)}, u32[]{:S(2)}) async-start(f32[1,6,2,128]{3,2,0,1:T(2,128)} %bitcast.73), calls=%async_computation.2 | async-start | bytes 12288 | tf_op jit(solution)/shard_map/all_to_all | solution.py:126
  195.9 1.3 all-to-all-done.2
  197.2 3.5 %all-to-all-start.1 = ((f32[1,6,2,128,128]{4,3,2,0,1:T(8,128)}), f32[1,6,2,128,128]{4,3,2,0,1:T(8,128)S(1)}, u32[]{:S(2)}, u32[]{:S(2)}) async-start(f32[1,6,2,128,128]{4,3,2,0,1:T(8,128)} %bitcast.71), calls=%async_computation.1 | async-start | bytes 1572864 | tf_op jit(solution)/shard_map/all_to_all | solution.py:127
  200.8 1.9 all-to-all-done.1
  (245 shorter events, 43.9 us)
Async XLA Ops:
  6.5 3.5 %copy-start.1 = (s32[2,1,16,9]{2,1,3,0:T(1,128)S(1)}, s32[2,1,16,9]{2,1,3,0:T(1,128)}, u32[]{:S(2)}) copy-start(s32[2,1,16,9]{2,1,3,0:T(1,128)} %param.11) | copy-start | bytes 3460
  6.5 3.6 %copy-start = (bf16[384,256]{1,0:T(8,128)(2,1)S(1)}, bf16[384,256]{1,0:T(8,128)(2,1)}, u32[]{:S(2)}) copy-start(bf16[384,256]{1,0:T(8,128)(2,1)} %param.8) | copy-start | bytes 589828
  6.5 49.9 %all-gather.3.cloned.1.call-start = ((), (), s32[]{:S(2)}) async-start(), calls=%async_computation.3 | async-start | bytes 1769472 | tf_op jit(solution)/shard_map/all_gather | solution.py:119
  8.3 92.9 %all-gather.5.cloned.1.call-start = ((), (), s32[]{:S(2)}) async-start(), calls=%async_computation.4 | async-start | bytes 1769472 | tf_op jit(solution)/shard_map/all_gather | solution.py:120
  192.6 4.6 %all-to-all-start.2 = ((f32[1,6,2,128]{3,2,0,1:T(2,128)}), f32[1,6,2,128]{3,2,0,1:T(2,128)S(1)}, u32[]{:S(2)}, u32[]{:S(2)}) async-start(f32[1,6,2,128]{3,2,0,1:T(2,128)} %bitcast.73), calls=%async_computation.2 | async-start | bytes 12288 | tf_op jit(solution)/shard_map/all_to_all | solution.py:126
  197.2 5.5 %all-to-all-start.1 = ((f32[1,6,2,128,128]{4,3,2,0,1:T(8,128)}), f32[1,6,2,128,128]{4,3,2,0,1:T(8,128)S(1)}, u32[]{:S(2)}, u32[]{:S(2)}) async-start(f32[1,6,2,128,128]{4,3,2,0,1:T(8,128)} %bitcast.71), calls=%async_computation.1 | async-start | bytes 1572864 | tf_op jit(solution)/shard_map/all_to_all | solution.py:127
Sparse Core Ops, SparseCore 0:
  9.5 46.8 all-gather.2
  58.6 42.5 all-gather.4
where the time goes:
time: 212 us; the launch traced here: 211 us
  waiting for transfers between devices  91.9 us (43%)
  local copies, waits for them, and re-layouts  44.8 us (21%)
  matrix products  42.9 us (20%)
  between operations  13.5 us (6%)
  starting transfers between devices  6.8 us (3%)
  blocking collectives  5.88 us (3%)
  other arithmetic  4.17 us (2%)
    all_gather x1, waiting for transfers between devices, local(): lax.all_gather(value_blocks, 'pb', axis=1, tiled=True)  44.8 us
    all_gather x1, waiting for transfers between devices, local(): lax.all_gather(key_blocks, 'pb', axis=1, tiled=True)  43.9 us
    dot_general x8, matrix products, attend_shard(): jnp.einsum('hsb,hsqd->bhqd', pair_flag, partial_output, precision=lax.Pre...  32.4 us
    gather x40, local copies, waits for them, and re-layouts, pick_blocks(): return jnp.take_along_axis(blocks, index[:, :, None, None], axis=1)  18.9 us
    dynamic_slice x16, local copies, waits for them, and re-layouts, one_shard(): lax.dynamic_slice_in_dim(value_piece, offset * partition_blocks, partitio...  8.53 us
    gather x24, local copies, waits for them, and re-layouts, attend_shard(): slot_peak = peak_new[query_index.T, head_numbers].transpose(1, 0, 2)  5.91 us
    dot_general x8, matrix products, attend_shard(): jnp.einsum('hsqd,hskd->hsqk', query_sel, key_sel, preferred_element_type=...  4.97 us
    dot_general x8, matrix products, attend_shard(): jnp.einsum('hsqk,hskd->hsqd', softmax_weight, value_sel, preferred_elemen...  4.42 us
  transfers between devices with their start and end apart: 4, of which 4 were waited for; matrix products, arithmetic and copies ran while one was open for 1% of the time, Pallas kernels for 0%

commit v1 on v0

v1 whole, which is shorter than its diff:
```python
import functools
import math

import jax
import jax.numpy as jnp
from jax import lax
from jax.experimental import pallas as pl
from jax.experimental.pallas import tpu as pltpu
from jax.sharding import PartitionSpec as P

HEAD = 128
HEADS = 2
BLOCK = 128
NEGATIVE_FILL = -1e30
EXP2_SCALE = HEAD ** (-0.5) * math.log2(math.e)
MESH = pl.DeviceIdType.MESH
LEFT, RIGHT, ACROSS = 0, 1, 2


def kernel(
    n_pb, n_ka, width, q_ref, k_ref, v_ref, pairs_ref, out_ref,
    qbuf, kbuf, vbuf, bias, peak, total, accum, obuf,
    send_sem, recv_sem, local_sem, swap_send, swap_recv,
):
    rows = q_ref.shape[0]
    tile = n_ka * rows
    cut = rows - BLOCK
    n_y = width
    n_z = n_pb // n_y
    core = lax.axis_index("ka")
    place = lax.axis_index("pb")
    z, y = place // n_y, place % n_y
    other = 1 - core
    across = z * n_y + (1 - y)
    has_left, has_right = z > 0, z < n_z - 1
    targets = {LEFT: place - n_y, RIGHT: place + n_y, ACROSS: across}

    barrier = pltpu.get_barrier_semaphore()
    pl.semaphore_signal(barrier, inc=1, device_id={"ka": other}, device_id_type=MESH)
    pl.semaphore_signal(barrier, inc=1, device_id={"pb": across}, device_id_type=MESH)

    @pl.when(has_left)
    def _():
        pl.semaphore_signal(barrier, inc=1, device_id={"pb": place - n_y}, device_id_type=MESH)

    @pl.when(has_right)
    def _():
        pl.semaphore_signal(barrier, inc=1, device_id={"pb": place + n_y}, device_id_type=MESH)

    my_columns = pl.ds(pl.multiple_of(core * HEAD, HEAD), HEAD)
    other_columns = pl.ds(pl.multiple_of(other * HEAD, HEAD), HEAD)
    my_rows = pl.ds(pl.multiple_of(core * rows, BLOCK), rows)
    other_rows = pl.ds(pl.multiple_of(other * rows, BLOCK), rows)

    stage = [
        pltpu.make_async_copy(k_ref.at[:, my_columns], kbuf.at[place, my_rows], local_sem.at[0]),
        pltpu.make_async_copy(v_ref.at[:, my_columns], vbuf.at[place, my_rows], local_sem.at[1]),
        pltpu.make_async_copy(q_ref.at[:, my_columns], qbuf.at[my_rows], local_sem.at[2]),
    ]
    for item in stage:
        item.start()

    codes = pairs_ref[core, 0]
    shards = codes.shape[0]
    query_block = lax.broadcasted_iota(jnp.int32, (shards, tile), 1) // BLOCK
    blocks = rows // BLOCK
    kept = [None] * blocks
    for slot in range(codes.shape[1]):
        column = jnp.broadcast_to(codes[:, slot : slot + 1], (shards, tile))
        for j in range(blocks):
            hit = column == query_block * blocks + j
            kept[j] = hit if kept[j] is None else kept[j] | hit
    for j in range(blocks):
        bias[j] = jnp.where(kept[j], 0.0, NEGATIVE_FILL).astype(jnp.float32)
    peak[...] = jnp.full_like(peak, NEGATIVE_FILL)
    total[...] = jnp.zeros_like(total)
    accum[...] = jnp.zeros_like(accum)

    pl.semaphore_wait(
        barrier, 2 + has_left.astype(jnp.int32) + has_right.astype(jnp.int32)
    )

    def swap(index, source, target):
        return pltpu.make_async_remote_copy(
            src_ref=source, dst_ref=target, send_sem=swap_send.at[index],
            recv_sem=swap_recv.at[index], device_id={"ka": other}, device_id_type=MESH,
        )

    swaps_out = [
        swap(0, k_ref.at[:, other_columns], kbuf.at[place, my_rows]),
        swap(1, v_ref.at[:, other_columns], vbuf.at[place, my_rows]),
        swap(2, q_ref.at[:, other_columns], qbuf.at[my_rows]),
    ]
    for item in swaps_out:
        item.start()

    def part(p, a, m):
        base = pl.multiple_of(a * rows, BLOCK)
        if m == 0:
            return kbuf.at[p, pl.ds(base, rows)]
        if m == 1:
            return vbuf.at[p, pl.ds(base, cut)]
        return vbuf.at[p, pl.ds(pl.multiple_of(base + cut, BLOCK), BLOCK)]

    def message(way, p, a, m):
        ref = part(p, a, m)
        return pltpu.make_async_remote_copy(
            src_ref=ref, dst_ref=ref, send_sem=send_sem.at[way, p, a, m],
            recv_sem=recv_sem.at[p, a, m], device_id={"pb": targets[way]}, device_id_type=MESH,
        )

    def send(way, p, a, m):
        if way == ACROSS:
            message(way, p, a, m).start()
        else:
            @pl.when(has_left if way == LEFT else has_right)
            def _():
                message(way, p, a, m).start()

    def arrive(p, a, m):
        message(ACROSS, p, a, m).wait_recv()

    def send_own(a, parts):
        for m in parts:
            for way in (ACROSS, LEFT, RIGHT):
                send(way, place, a, m)

    stage[0].wait()
    send_own(core, (0,))
    stage[1].wait()
    send_own(core, (2, 1))
    swap(0, k_ref.at[:, other_columns], kbuf.at[place, other_rows]).wait_recv()
    send_own(other, (0,))
    swap(1, v_ref.at[:, other_columns], vbuf.at[place, other_rows]).wait_recv()
    send_own(other, (2, 1))
    stage[2].wait()
    swap(2, q_ref.at[:, other_columns], qbuf.at[other_rows]).wait_recv()

    lanes = 256 if tile % 256 == 0 else 128

    def attend(p):
        for start in range(0, tile, lanes):
            span = pl.ds(start, lanes)
            scores = lax.dot_general(
                kbuf[p], qbuf[span, :], (((1,), (1,)), ((), ())),
                preferred_element_type=jnp.float32,
            )
            masked = []
            for a in range(n_ka):
                for j in range(blocks):
                    row = (a * blocks + j) * BLOCK
                    line = bias[j, pl.ds(p * n_ka + a, 1), span]
                    masked.append(scores[row : row + BLOCK] + line)
            scores = jnp.concatenate(masked, axis=0)
            before = peak[:, span]
            after = jnp.maximum(before, scores.max(0, keepdims=True))
            rescale = jnp.exp2((before - after) * EXP2_SCALE)
            chances = jnp.exp2((scores - after) * EXP2_SCALE)
            peak[:, span] = after
            total[:, span] = total[:, span] * rescale + chances.sum(0, keepdims=True)
            accum[:, span] = accum[:, span] * rescale + lax.dot_general(
                vbuf[p], chances.astype(jnp.bfloat16), (((0,), (0,)), ((), ())),
                preferred_element_type=jnp.float32,
            )

    attend(place)

    for a in range(n_ka):
        arrive(across, a, 2)
        send(LEFT, across, a, 2)
        send(RIGHT, across, a, 2)

    def sides(step):
        return ((z - step, z - step >= 0, RIGHT), (z + step, z + step < n_z, LEFT))

    def attend_across(p):
        for a in range(n_ka):
            arrive(p, a, 0)
            arrive(p, a, 1)
        attend(p)

    def forward(step):
        for a in range(n_ka):
            for m in (0, 1):
                for far, valid, way in sides(step):
                    @pl.when(valid)
                    def _(far=far, way=way):
                        p = far * n_y + y
                        arrive(p, a, m)
                        send(way, p, a, m)
                        send(ACROSS, p, a, m)
            for far, valid, way in sides(step):
                @pl.when(valid)
                def _(far=far, way=way):
                    for near in (y, 1 - y):
                        p = far * n_y + near
                        arrive(p, a, 2)
                        send(way, p, a, 2)

    forward(1)
    attend_across(across)

    def one_step(step, carry):
        for far, valid, _ in sides(step):
            @pl.when(valid)
            def _(far=far):
                attend(far * n_y + y)

        @pl.when(step < n_z - 1)
        def _():
            forward(step + 1)

        for far, valid, _ in sides(step):
            @pl.when(valid)
            def _(far=far):
                attend_across(far * n_y + 1 - y)
        return carry

    lax.fori_loop(1, n_z, one_step, 0)

    def finish(which):
        span = pl.ds(pl.multiple_of(which * rows, BLOCK), rows)
        done = accum[:, span] / total[:, span]
        obuf[span, :] = done.T.astype(obuf.dtype)

    finish(other)
    give = pltpu.make_async_remote_copy(
        src_ref=obuf.at[other_rows], dst_ref=out_ref.at[:, my_columns],
        send_sem=swap_send.at[3], recv_sem=swap_recv.at[3],
        device_id={"ka": other}, device_id_type=MESH,
    )
    give.start()
    finish(core)
    keep = pltpu.make_async_copy(obuf.at[my_rows], out_ref.at[:, my_columns], local_sem.at[3])
    keep.start()

    def drain(way, far, near, a, m):
        message(way, far * n_y + near, a, m).wait_send()

    def drain_line(way):
        def body(far, carry):
            for a in range(n_ka):
                for m in (0, 1):
                    drain(way, far, y, a, m)
                for near in range(n_y):
                    drain(way, far, near, a, 2)
            return carry
        return body

    lax.fori_loop(jnp.where(has_left, z, n_z), n_z, drain_line(LEFT), 0)
    lax.fori_loop(0, jnp.where(has_right, z + 1, 0), drain_line(RIGHT), 0)

    def drain_across(far, carry):
        for a in range(n_ka):
            for m in (0, 1):
                drain(ACROSS, far, y, a, m)
        return carry

    lax.fori_loop(0, n_z, drain_across, 0)
    for a in range(n_ka):
        drain(ACROSS, z, y, a, 2)
    for item in swaps_out:
        item.wait_send()
    give.wait_send()
    keep.wait()
    pltpu.make_async_remote_copy(
        src_ref=obuf.at[other_rows], dst_ref=out_ref.at[:, other_columns],
        send_sem=swap_send.at[3], recv_sem=swap_recv.at[3],
        device_id={"ka": other}, device_id_type=MESH,
    ).wait_recv()


def solution(mesh):
    n_pb, n_ka = mesh.shape["pb"], mesh.shape["ka"]
    width = 2

    def local(queries, keys, values, block_pairs):
        rows = queries.shape[0]
        tile = n_ka * rows
        shards = block_pairs.shape[2]
        anywhere = pl.BlockSpec(memory_space=pl.ANY)
        return pl.pallas_call(
            functools.partial(kernel, n_pb, n_ka, width),
            out_shape=jax.ShapeDtypeStruct(queries.shape, queries.dtype),
            in_specs=[anywhere, anywhere, anywhere, pl.BlockSpec(memory_space=pltpu.VMEM)],
            out_specs=anywhere,
            scratch_shapes=[
                pltpu.VMEM((tile, HEAD), jnp.bfloat16),
                pltpu.VMEM((n_pb, tile, HEAD), jnp.bfloat16),
                pltpu.VMEM((n_pb, tile, HEAD), jnp.bfloat16),
                pltpu.VMEM((rows // BLOCK, shards, tile), jnp.float32),
                pltpu.VMEM((1, tile), jnp.float32),
                pltpu.VMEM((1, tile), jnp.float32),
                pltpu.VMEM((HEAD, tile), jnp.float32),
                pltpu.VMEM((tile, HEAD), jnp.bfloat16),
                pltpu.SemaphoreType.DMA((3, n_pb, n_ka, 3)),
                pltpu.SemaphoreType.DMA((n_pb, n_ka, 3)),
                pltpu.SemaphoreType.DMA((4,)),
                pltpu.SemaphoreType.DMA((4,)),
                pltpu.SemaphoreType.DMA((4,)),
            ],
            compiler_params=pltpu.CompilerParams(collective_id=0, has_side_effects=True),
        )(queries, keys, values, block_pairs)

    rows_spec = P(("groups", "pb", "ka"), None)
    return jax.shard_map(
        local, mesh=mesh,
        in_specs=(rows_spec, rows_spec, rows_spec, P("groups", "pb", None, None)),
        out_specs=rows_spec, check_vma=False,
    )
```

time: 212 us -> 46.6 us (0.22)
  waiting for transfers between devices: 91.9 us -> 0 us
  Pallas kernels: 0 us -> 43.3 us
  matrix products: 42.9 us -> 0 us
  local copies, waits for them, and re-layouts: 44.8 us -> 3 us
  between operations: 13.5 us -> 0.01 us
  starting transfers between devices: 6.8 us -> 0 us
  blocking collectives: 5.88 us -> 0 us
  other arithmetic: 4.17 us -> 0 us
    all_gather x2 -> x0, waiting for transfers between devices: 88.6 us -> none  [the longest x1 44.8 us: local(): lax.all_gather(value_blocks, 'pb', axis=1, tiled=True)]
    pallas_call x0 -> x1, Pallas kernels: none -> 43.3 us  [local(): pl.pallas_call(functools.partial(kernel, n_pb, n_ka, width), out_shape=ja...]
    dot_general x32 -> x0, matrix products: 42.9 us -> none  [the longest x8 32.4 us: attend_shard(): jnp.einsum('hsb,hsqd->bhqd', pair_flag, partial_output, precision=lax.Pre...]
    gather x64 -> x0, local copies, waits for them, and re-layouts: 24.8 us -> none  [the longest x40 18.9 us: pick_blocks(): return jnp.take_along_axis(blocks, index[:, :, None, None], axis=1)]
    dynamic_slice x33 -> x0, local copies, waits for them, and re-layouts: 8.71 us -> none  [the longest x16 8.53 us: one_shard(): lax.dynamic_slice_in_dim(value_piece, offset * partition_blocks, partitio...]
    all_to_all x2 -> x0, starting transfers between devices: 6.76 us -> none  [the longest x1 3.53 us: local(): lax.all_to_all(accum_end[None], 'ka', split_axis=1, concat_axis=0, tiled=...]
    all_to_all x1 -> x0, blocking collectives: 3.69 us -> none  [local(): lax.all_to_all(peak_end[None], 'ka', split_axis=1, concat_axis=0, tiled=T...]
    all_to_all x2 -> x0, waiting for transfers between devices: 3.23 us -> none  [the longest x1 1.89 us: local(): lax.all_to_all(accum_end[None], 'ka', split_axis=1, concat_axis=0, tiled=...]
  transfers between devices with their start and end apart: 4 -> 0, of which waited for: 4 -> 0; matrix products, arithmetic and copies ran while one was open for 1% -> 0% of each run, Pallas kernels for 0% -> 0%
where the time goes in v1:
time: 46.6 us; the launch traced here: 46.3 us
  Pallas kernels  43.3 us (93%)
  local copies, waits for them, and re-layouts  3 us (6%)
    pallas_call x1, Pallas kernels, local(): pl.pallas_call(functools.partial(kernel, n_pb, n_ka, width), out_shape=ja...  43.3 us
    unnamed x2, local copies, waits for them, and re-layouts  3 us

profile of v1, /device:TPU:0, one launch (start us, length us, event | category | flops | bytes accessed | tf_op | source)
XLA Modules:
  0.0 46.3 jit_solution(12973250848176364686)
XLA Ops:
  0.0 1.4 %copy.5.pairs_ref = s32[2,1,16,9]{3,2,1,0:T(8,128)} copy(s32[2,1,16,9]{2,1,3,0:T(1,128)} %param.7) | data formatting | bytes 2304 | tf_op args[3]
  1.4 43.3 %shard_map.46 = bf16[384,256]{1,0:T(8,128)(2,1)} custom-call(bf16[384,256]{1,0:T(8,128)(2,1)} %q_ref.1, bf16[384,256]{1,0:T(8,128)(2,1)} %k_ref.1, bf16[384,256]{1,0:T(8,128)(2,1)} %v_ref.1, s32[2,1,16,9]{3,2,1,0:T(8,128)} %copy.5.pairs_ref), custom_call_target="tpu_custom_call" | custom-call | tf_op jit(solution)/shard_map/pallas_call | solution.py:282
  44.7 1.6 %copy.7 = bf16[384,256]{1,0:T(8,128)(2,1)} copy(bf16[384,256]{1,0:T(8,128)(2,1)} %shard_map.46) | data formatting | bytes 393216

commit v2 on v1

--- a/solution.py
+++ b/solution.py
@@ -19,12 +19,13 @@
 
 def kernel(
     n_pb, n_ka, width, q_ref, k_ref, v_ref, pairs_ref, out_ref,
-    qbuf, kbuf, vbuf, bias, peak, total, accum, obuf,
+    qbuf, kbuf, vbuf, bias, peak, total, accum, obuf, qturned,
     send_sem, recv_sem, local_sem, swap_send, swap_recv,
 ):
     rows = q_ref.shape[0]
     tile = n_ka * rows
-    cut = rows - BLOCK
+    late = BLOCK - BLOCK // 4
+    half = (rows - late) // 2
     n_y = width
     n_z = n_pb // n_y
     core = lax.axis_index("ka")
@@ -60,7 +61,62 @@
     for item in stage:
         item.start()
 
-    codes = pairs_ref[core, 0]
+    pl.semaphore_wait(
+        barrier, 2 + has_left.astype(jnp.int32) + has_right.astype(jnp.int32)
+    )
+
+    def swap(index, source, target):
+        return pltpu.make_async_remote_copy(
+            src_ref=source, dst_ref=target, send_sem=swap_send.at[index],
+            recv_sem=swap_recv.at[index], device_id={"ka": other}, device_id_type=MESH,
+        )
+
+    swaps_out = [
+        swap(0, k_ref.at[:, other_columns], kbuf.at[place, my_rows]),
+        swap(1, v_ref.at[:, other_columns], vbuf.at[place, my_rows]),
+        swap(2, q_ref.at[:, other_columns], qbuf.at[my_rows]),
+    ]
+    for item in swaps_out:
+        item.start()
+
+    spans = ((0, rows), (0, half), (half, half), (2 * half, late))
+    early, last = (0, 1, 2), 3
+
+    def part(p, a, m):
+        start, size = spans[m]
+        span = pl.ds(pl.multiple_of(a * rows + start, 16), size)
+        return (vbuf if m else kbuf).at[p, span]
+
+    def message(way, p, a, m, source=None):
+        ref = part(p, a, m)
+        return pltpu.make_async_remote_copy(
+            src_ref=ref if source is None else source, dst_ref=ref, send_sem=send_sem.at[way, p, a, m],
+            recv_sem=recv_sem.at[p, a, m], device_id={"pb": targets[way]}, device_id_type=MESH,
+        )
+
+    def send(way, p, a, m, source=None):
+        if way == ACROSS:
+            message(way, p, a, m, source).start()
+        else:
+            @pl.when(has_left if way == LEFT else has_right)
+            def _():
+                message(way, p, a, m, source).start()
+
+    def arrive(p, a, m):
+        message(ACROSS, p, a, m).wait_recv()
+
+    def send_own(a, parts, source=None, ways=(ACROSS, LEFT, RIGHT)):
+        for m in parts:
+            start, size = spans[m]
+            view = None if source is None else source.at[pl.ds(start, size), my_columns]
+            for way in ways:
+                send(way, place, a, m, view)
+
+    send_own(core, (0,), k_ref)
+    send_own(core, (last,), v_ref, (ACROSS,))
+    send_own(core, (1, 2), v_ref)
+
+    codes = pairs_ref[core, :, 0, :].T
     shards = codes.shape[0]
     query_block = lax.broadcasted_iota(jnp.int32, (shards, tile), 1) // BLOCK
     blocks = rows // BLOCK
@@ -76,80 +132,34 @@
     total[...] = jnp.zeros_like(total)
     accum[...] = jnp.zeros_like(accum)
 
-    pl.semaphore_wait(
-        barrier, 2 + has_left.astype(jnp.int32) + has_right.astype(jnp.int32)
-    )
-
-    def swap(index, source, target):
-        return pltpu.make_async_remote_copy(
-            src_ref=source, dst_ref=target, send_sem=swap_send.at[index],
-            recv_sem=swap_recv.at[index], device_id={"ka": other}, device_id_type=MESH,
-        )
-
-    swaps_out = [
-        swap(0, k_ref.at[:, other_columns], kbuf.at[place, my_rows]),
-        swap(1, v_ref.at[:, other_columns], vbuf.at[place, my_rows]),
-        swap(2, q_ref.at[:, other_columns], qbuf.at[my_rows]),
-    ]
-    for item in swaps_out:
-        item.start()
-
-    def part(p, a, m):
-        base = pl.multiple_of(a * rows, BLOCK)
-        if m == 0:
-            return kbuf.at[p, pl.ds(base, rows)]
-        if m == 1:
-            return vbuf.at[p, pl.ds(base, cut)]
-        return vbuf.at[p, pl.ds(pl.multiple_of(base + cut, BLOCK), BLOCK)]
-
-    def message(way, p, a, m):
-        ref = part(p, a, m)
-        return pltpu.make_async_remote_copy(
-            src_ref=ref, dst_ref=ref, send_sem=send_sem.at[way, p, a, m],
-            recv_sem=recv_sem.at[p, a, m], device_id={"pb": targets[way]}, device_id_type=MESH,
-        )
-
-    def send(way, p, a, m):
-        if way == ACROSS:
-            message(way, p, a, m).start()
-        else:
-            @pl.when(has_left if way == LEFT else has_right)
-            def _():
-                message(way, p, a, m).start()
-
-    def arrive(p, a, m):
-        message(ACROSS, p, a, m).wait_recv()
-
-    def send_own(a, parts):
-        for m in parts:
-            for way in (ACROSS, LEFT, RIGHT):
-                send(way, place, a, m)
-
-    stage[0].wait()
-    send_own(core, (0,))
-    stage[1].wait()
-    send_own(core, (2, 1))
     swap(0, k_ref.at[:, other_columns], kbuf.at[place, other_rows]).wait_recv()
     send_own(other, (0,))
     swap(1, v_ref.at[:, other_columns], vbuf.at[place, other_rows]).wait_recv()
-    send_own(other, (2, 1))
-    stage[2].wait()
+    send_own(other, (last,), None, (ACROSS,))
+    send_own(other, (1, 2))
+    send_own(core, (last,), v_ref, (LEFT, RIGHT))
+    send_own(other, (last,), None, (LEFT, RIGHT))
+    for item in stage:
+        item.wait()
     swap(2, q_ref.at[:, other_columns], qbuf.at[other_rows]).wait_recv()
 
-    lanes = 256 if tile % 256 == 0 else 128
-
-    def attend(p):
+    qturned[...] = qbuf[...].T
+    lanes = tile
+
+    def attend(p, first=0, count=n_ka):
+        keys = pl.ds(first * rows, count * rows)
+        turned = vbuf[p, keys].T
         for start in range(0, tile, lanes):
             span = pl.ds(start, lanes)
             scores = lax.dot_general(
-                kbuf[p], qbuf[span, :], (((1,), (1,)), ((), ())),
+                kbuf[p, keys], qturned[:, span], (((1,), (0,)), ((), ())),
                 preferred_element_type=jnp.float32,
             )
             masked = []
-            for a in range(n_ka):
+            for a in range(count):
                 for j in range(blocks):
                     row = (a * blocks + j) * BLOCK
-                    line = bias[j, pl.ds(p * n_ka + a, 1), span]
+                    line = bias[j, pl.ds(p * n_ka + first + a, 1), span]
                     masked.append(scores[row : row + BLOCK] + line)
             scores = jnp.concatenate(masked, axis=0)
             before = peak[:, span]
@@ -159,29 +169,29 @@
             peak[:, span] = after
             total[:, span] = total[:, span] * rescale + chances.sum(0, keepdims=True)
             accum[:, span] = accum[:, span] * rescale + lax.dot_general(
-                vbuf[p], chances.astype(jnp.bfloat16), (((0,), (0,)), ((), ())),
+                turned, chances.astype(jnp.bfloat16), (((1,), (0,)), ((), ())),
                 preferred_element_type=jnp.float32,
             )
 
     attend(place)
 
     for a in range(n_ka):
-        arrive(across, a, 2)
-        send(LEFT, across, a, 2)
-        send(RIGHT, across, a, 2)
+        arrive(across, a, last)
+        send(LEFT, across, a, last)
+        send(RIGHT, across, a, last)
 
     def sides(step):
         return ((z - step, z - step >= 0, RIGHT), (z + step, z + step < n_z, LEFT))
 
     def attend_across(p):
         for a in range(n_ka):
-            arrive(p, a, 0)
-            arrive(p, a, 1)
+            for m in early:
+                arrive(p, a, m)
         attend(p)
 
-    def forward(step):
+    def forward_early(step):
         for a in range(n_ka):
-            for m in (0, 1):
+            for m in early:
                 for far, valid, way in sides(step):
                     @pl.when(valid)
                     def _(far=far, way=way):
@@ -189,15 +199,26 @@
                         arrive(p, a, m)
                         send(way, p, a, m)
                         send(ACROSS, p, a, m)
+
+    def forward_last(step):
+        for a in range(n_ka):
             for far, valid, way in sides(step):
                 @pl.when(valid)
                 def _(far=far, way=way):
                     for near in (y, 1 - y):
                         p = far * n_y + near
-                        arrive(p, a, 2)
-                        send(way, p, a, 2)
-
-    forward(1)
+                        arrive(p, a, last)
+                        send(way, p, a, last)
+
+    def across_sides(step):
+        for far, valid, _ in sides(step):
+            @pl.when(valid)
+            def _(far=far):
+                attend_across(far * n_y + 1 - y)
+
+    at_end = jnp.logical_not(jnp.logical_and(has_left, has_right))
+    forward_early(1)
+    forward_last(1)
     attend_across(across)
 
     def one_step(step, carry):
@@ -208,12 +229,19 @@
 
         @pl.when(step < n_z - 1)
         def _():
-            forward(step + 1)
-
-        for far, valid, _ in sides(step):
-            @pl.when(valid)
-            def _(far=far):
-                attend_across(far * n_y + 1 - y)
+            forward_early(step + 1)
+
+        @pl.when(at_end)
+        def _():
+            across_sides(step)
+
+        @pl.when(step < n_z - 1)
+        def _():
+            forward_last(step + 1)
+
+        @pl.when(jnp.logical_not(at_end))
+        def _():
+            across_sides(step)
         return carry
 
     lax.fori_loop(1, n_z, one_step, 0)
@@ -240,10 +268,10 @@
     def drain_line(way):
         def body(far, carry):
             for a in range(n_ka):
-                for m in (0, 1):
+                for m in early:
                     drain(way, far, y, a, m)
                 for near in range(n_y):
-                    drain(way, far, near, a, 2)
+                    drain(way, far, near, a, last)
             return carry
         return body
 
@@ -252,13 +280,13 @@
 
     def drain_across(far, carry):
         for a in range(n_ka):
-            for m in (0, 1):
+            for m in early:
                 drain(ACROSS, far, y, a, m)
         return carry
 
     lax.fori_loop(0, n_z, drain_across, 0)
     for a in range(n_ka):
-        drain(ACROSS, z, y, a, 2)
+        drain(ACROSS, z, y, a, last)
     for item in swaps_out:
         item.wait_send()
     give.wait_send()
@@ -293,14 +321,15 @@
                 pltpu.VMEM((1, tile), jnp.float32),
                 pltpu.VMEM((HEAD, tile), jnp.float32),
                 pltpu.VMEM((tile, HEAD), jnp.bfloat16),
-                pltpu.SemaphoreType.DMA((3, n_pb, n_ka, 3)),
-                pltpu.SemaphoreType.DMA((n_pb, n_ka, 3)),
+                pltpu.VMEM((HEAD, tile), jnp.bfloat16),
+                pltpu.SemaphoreType.DMA((3, n_pb, n_ka, 4)),
+                pltpu.SemaphoreType.DMA((n_pb, n_ka, 4)),
                 pltpu.SemaphoreType.DMA((4,)),
                 pltpu.SemaphoreType.DMA((4,)),
                 pltpu.SemaphoreType.DMA((4,)),
             ],
             compiler_params=pltpu.CompilerParams(collective_id=0, has_side_effects=True),
-        )(queries, keys, values, block_pairs)
+        )(queries, keys, values, block_pairs.transpose(0, 3, 1, 2))
 
     rows_spec = P(("groups", "pb", "ka"), None)
     return jax.shard_map(

time: 46.6 us -> 43.6 us (0.936)
  Pallas kernels: 43.3 us -> 41.7 us
  local copies, waits for them, and re-layouts: 3 us -> 1.62 us
    pallas_call x1, Pallas kernels: 43.3 us -> 41.7 us  [local(): pl.pallas_call(functools.partial(kernel, n_pb, n_ka, width), out_shape=ja...]
    unnamed x2 -> x1, local copies, waits for them, and re-layouts: 3 us -> 1.62 us
where the time goes in v2:
time: 43.6 us; the launch traced here: 43.4 us
  Pallas kernels  41.7 us (96%)
  local copies, waits for them, and re-layouts  1.62 us (4%)
    pallas_call x1, Pallas kernels, local(): pl.pallas_call(functools.partial(kernel, n_pb, n_ka, width), out_shape=ja...  41.7 us
    unnamed x1, local copies, waits for them, and re-layouts  1.62 us

profile of v2, /device:TPU:0, one launch (start us, length us, event | category | flops | bytes accessed | tf_op | source)
XLA Modules:
  0.0 43.4 jit_solution(18326350609886087055)
XLA Ops:
  0.0 41.7 %shard_map.46 = bf16[384,256]{1,0:T(8,128)(2,1)} custom-call(bf16[384,256]{1,0:T(8,128)(2,1)} %q_ref.1, bf16[384,256]{1,0:T(8,128)(2,1)} %k_ref.1, bf16[384,256]{1,0:T(8,128)(2,1)} %v_ref.1, s32[2,9,1,16]{3,2,1,0:T(1,128)} %bitcast.1), custom_call_target="tpu_custom_call" | custom-call | tf_op jit(solution)/shard_map/pallas_call | solution.py:310
  41.8 1.6 %copy.6 = bf16[384,256]{1,0:T(8,128)(2,1)} copy(bf16[384,256]{1,0:T(8,128)(2,1)} %shard_map.46) | data formatting | bytes 393216

commit v3 on v2

--- a/solution.py
+++ b/solution.py
@@ -116,6 +116,13 @@
     send_own(core, (last,), v_ref, (ACROSS,))
     send_own(core, (1, 2), v_ref)
 
+    swap(0, k_ref.at[:, other_columns], kbuf.at[place, other_rows]).wait_recv()
+    send_own(other, (0,))
+    swap(1, v_ref.at[:, other_columns], vbuf.at[place, other_rows]).wait_recv()
+    send_own(other, (last,), None, (ACROSS,))
+    send_own(other, (1, 2))
+    send_own(core, (last,), v_ref, (LEFT, RIGHT))
+    send_own(other, (last,), None, (LEFT, RIGHT))
     codes = pairs_ref[core, :, 0, :].T
     shards = codes.shape[0]
     query_block = lax.broadcasted_iota(jnp.int32, (shards, tile), 1) // BLOCK
@@ -132,13 +139,6 @@
     total[...] = jnp.zeros_like(total)
     accum[...] = jnp.zeros_like(accum)
 
-    swap(0, k_ref.at[:, other_columns], kbuf.at[place, other_rows]).wait_recv()
-    send_own(other, (0,))
-    swap(1, v_ref.at[:, other_columns], vbuf.at[place, other_rows]).wait_recv()
-    send_own(other, (last,), None, (ACROSS,))
-    send_own(other, (1, 2))
-    send_own(core, (last,), v_ref, (LEFT, RIGHT))
-    send_own(other, (last,), None, (LEFT, RIGHT))
     for item in stage:
         item.wait()
     swap(2, q_ref.at[:, other_columns], qbuf.at[other_rows]).wait_recv()
@@ -216,16 +216,21 @@
             def _(far=far):
                 attend_across(far * n_y + 1 - y)
 
+    def near_sides(step):
+        for far, valid, _ in sides(step):
+            @pl.when(valid)
+            def _(far=far):
+                attend(far * n_y + y)
+
     at_end = jnp.logical_not(jnp.logical_and(has_left, has_right))
     forward_early(1)
     forward_last(1)
     attend_across(across)
 
     def one_step(step, carry):
-        for far, valid, _ in sides(step):
-            @pl.when(valid)
-            def _(far=far):
-                attend(far * n_y + y)
+        @pl.when(at_end)
+        def _():
+            near_sides(step)
 
         @pl.when(step < n_z - 1)
         def _():
@@ -241,6 +246,7 @@
 
         @pl.when(jnp.logical_not(at_end))
         def _():
+            near_sides(step)
             across_sides(step)
         return carry
 

time: 43.6 us -> 43.6 us (level)
  no operation moved by 1% of the time
where the time goes in v3:
time: 43.6 us; the launch traced here: 43.4 us
  Pallas kernels  41.7 us (96%)
  local copies, waits for them, and re-layouts  1.62 us (4%)
    pallas_call x1, Pallas kernels, local(): pl.pallas_call(functools.partial(kernel, n_pb, n_ka, width), out_shape=ja...  41.7 us
    unnamed x1, local copies, waits for them, and re-layouts  1.62 us

profile of v3, /device:TPU:0, one launch (start us, length us, event | category | flops | bytes accessed | tf_op | source)
XLA Modules:
  0.0 43.4 jit_solution(1066461577944592261)
XLA Ops:
  0.0 41.7 %shard_map.46 = bf16[384,256]{1,0:T(8,128)(2,1)} custom-call(bf16[384,256]{1,0:T(8,128)(2,1)} %q_ref.1, bf16[384,256]{1,0:T(8,128)(2,1)} %k_ref.1, bf16[384,256]{1,0:T(8,128)(2,1)} %v_ref.1, s32[2,9,1,16]{3,2,1,0:T(1,128)} %bitcast.1), custom_call_target="tpu_custom_call" | custom-call | tf_op jit(solution)/shard_map/pallas_call | solution.py:316
  41.8 1.6 %copy.6 = bf16[384,256]{1,0:T(8,128)(2,1)} copy(bf16[384,256]{1,0:T(8,128)(2,1)} %shard_map.46) | data formatting | bytes 393216
